TPU v7x, 32 devices: a whole 2x2x4 slice. The times are simulated.
32 devices in a mesh: groups: 2 (over x), seq: 8 (over z, y), tensor: 2 (over core).
Axes of the slice: x: 2, y: 2, z: 4, core: 2. Of those that a mesh axis runs over, the one named last changes fastest.
Arguments:
- inputs: bfloat16 [4096, 1536], P(('groups', 'seq'), 'tensor'), parts along dimension 0, may hold values from -6 to 6
- w_dilated: bfloat16 [1536, 3, 1536], P(None, None, 'tensor'), may hold values from -0.09375 to 0.09375
- w_point: bfloat16 [1536, 1536], P(None, 'tensor'), may hold values from -0.15625 to 0.15625
- cotangent: bfloat16 [4096, 1536], P(('groups', 'seq'), 'tensor'), parts along dimension 0, may hold values from -6 to 6
Outputs:
- output: bfloat16 [4096, 1536], P(('groups', 'seq'), 'tensor'), parts along dimension 0
- grad_inputs: bfloat16 [4096, 1536], P(('groups', 'seq'), 'tensor'), parts along dimension 0
- grad_point: float32 [3072, 1536], P(('groups', 'seq'), 'tensor'), parts along dimension 0
There are 2 independent parts, one for each index of `groups`. A program takes and returns all parts, laid end to end along the dimension named above; an argument that names none is the same for every part. Nothing has to cross between parts.
All inputs are finite; a program needn't handle non-finite values.
Results may differ from a plain program's by a relative error of at most 0.007.
Values may be sent and summed in bfloat16 or wider, within the bound.
A program may use at most 64 MiB of HBM per device.

v0:
```python
import math

import jax
import jax.numpy as jnp
from jax import lax
from jax.sharding import PartitionSpec as P

DILATION_BINS = 32


gelu_cubic = 0.044715
gelu_scale = math.sqrt(2.0 / math.pi)


def extended(block, sides, width):
    for axis, dim in sides:
        count = lax.axis_size(axis)
        forward = [(i, i + 1) for i in range(count - 1)]
        backward = [(target, source) for source, target in forward]
        low = lax.ppermute(
            lax.slice_in_dim(block, block.shape[dim] - width, None, axis=dim), axis, forward
        )
        high = lax.ppermute(lax.slice_in_dim(block, 0, width, axis=dim), axis, backward)
        block = jnp.concatenate([low, block, high], axis=dim)
    return block


def gelu_pair(values):
    inner = gelu_scale * (values + gelu_cubic * values * values * values)
    tangent = jnp.tanh(inner)
    result = 0.5 * values * (1.0 + tangent)
    derivative = 0.5 * (1.0 + tangent) + 0.5 * values * (1.0 - tangent * tangent) * gelu_scale * (
        1.0 + 3.0 * gelu_cubic * values * values
    )
    return (result, derivative)


def local(inputs, w_dilated, w_point, cotangent):
    sequence_rows = inputs.shape[0]
    rimmed = extended(inputs, (("seq", 0),), DILATION_BINS)
    padded_input = lax.all_gather(rimmed, "tensor", axis=1, tiled=True)
    displaced_rows = jnp.stack(
        [
            padded_input[
                kernel_tap_index * DILATION_BINS : kernel_tap_index * DILATION_BINS + sequence_rows
            ]
            for kernel_tap_index in range(3)
        ],
        axis=1,
    )
    hidden = jnp.einsum(
        "tkc,cko->to", displaced_rows, w_dilated, preferred_element_type=jnp.float32
    )
    activation, derivative = gelu_pair(hidden)
    activation = activation.astype(jnp.bfloat16)
    mixed_terms = jnp.einsum("tc,oc->to", activation, w_point, preferred_element_type=jnp.float32)
    mixed_sum = lax.psum_scatter(
        mixed_terms.astype(jnp.bfloat16), "tensor", scatter_dimension=1, tiled=True
    ).astype(jnp.float32)
    output = (inputs.astype(jnp.float32) + mixed_sum).astype(jnp.bfloat16)
    full_grad = lax.all_gather(cotangent, "tensor", axis=1, tiled=True)
    grad_act = jnp.dot(full_grad, w_point, preferred_element_type=jnp.float32)
    hidden_gradient = (grad_act * derivative).astype(jnp.bfloat16)
    padded_gradient = extended(hidden_gradient, (("seq", 0),), DILATION_BINS)
    back_taps = jnp.stack(
        [
            padded_gradient[
                (2 - kernel_tap_index) * DILATION_BINS : (2 - kernel_tap_index) * DILATION_BINS
                + sequence_rows
            ]
            for kernel_tap_index in range(3)
        ],
        axis=1,
    )
    back_terms = jnp.einsum("tko,cko->tc", back_taps, w_dilated, preferred_element_type=jnp.float32)
    back_sum = lax.psum_scatter(
        back_terms.astype(jnp.bfloat16), "tensor", scatter_dimension=1, tiled=True
    ).astype(jnp.float32)
    grad_inputs = (cotangent.astype(jnp.float32) + back_sum).astype(jnp.bfloat16)
    grad_point = lax.psum_scatter(
        jnp.einsum("to,tc->oc", full_grad, activation, preferred_element_type=jnp.float32),
        "seq",
        scatter_dimension=0,
        tiled=True,
    )
    return (output, grad_inputs, grad_point)


def solution(mesh):
    placed = (
        P(("groups", "seq"), "tensor"),
        P(None, None, "tensor"),
        P(None, "tensor"),
        P(("groups", "seq"), "tensor"),
    )
    return jax.shard_map(
        local,
        mesh=mesh,
        in_specs=placed,
        out_specs=(
            P(("groups", "seq"), "tensor"),
            P(("groups", "seq"), "tensor"),
            P(("groups", "seq"), "tensor"),
        ),
        check_vma=False,
    )
```

profile of v0, /device:TPU:0, one launch (start us, length us, event | category | flops | bytes accessed | tf_op | source)
XLA Modules:
  0.0 164.7 jit_solution(2448925915653958948)
XLA Ops:
  7.2 1.0 fusion.26
  8.2 4.9 %collective-permute-start = (bf16[32,768]{1,0:T(8,128)(2,1)S(1)}, bf16[32,768]{1,0:T(8,128)(2,1)S(1)}, u32[]{:S(2)}, u32[]{:S(2)}) collective-permute-start(bf16[32,768]{1,0:T(8,128)(2,1)S(1)} %get-tuple-element.16), channel_id=1, source_target_pairs={{0,2},{2,4},{4,6},{6,8},{8,10},{10,12},{12,14},{1,3},{3,5},{5,7},{... | collective-permute-start | bytes 147464 | tf_op jit(solution)/shard_map/ppermute | solution.py:20
  13.1 1.3 collective-permute-start.1
  14.4 0.4 collective-permute-done
  14.8 4.3 %collective-permute-done.1 = bf16[32,768]{1,0:T(8,128)(2,1)S(1)} collective-permute-done((bf16[32,768]{1,0:T(8,128)(2,1)S(1)}, bf16[32,768]{1,0:T(8,128)(2,1)S(1)}, u32[]{:S(2)}, u32[]{:S(2)}) %collective-permute-start.1) | collective-permute-done | bytes 49184 | tf_op jit(solution)/shard_map/ppermute | solution.py:23
  19.1 1.2 pad_maximum_fusion
  20.2 2.6 %all_gather.6 = bf16[320,1536]{1,0:T(8,128)(2,1)S(1)} all-gather(bf16[320,768]{1,0:T(8,128)(2,1)S(1)} %pad_maximum_fusion), channel_id=1, replica_groups=mesh['groups'=2,'seq'=8,'tensor'=2] {'tensor'}, dimensions={1}, use_global_device_ids=true | all-gather | bytes 1474560 | tf_op jit(solution)/shard_map/all_gather | solution.py:41
  22.9 0.2 slice_bitcast_fusion.2
  23.1 2.0 %fusion.7 = f32[256,768]{1,0:T(8,128)S(1)} fusion(bf16[1536,3,768]{2,0,1:T(8,128)(2,1)S(1)} %copy-done.4, bf16[256,1,1536]{2,0,1:T(8,128)(2,1)S(1)} %get-tuple-element.10, bf16[256,1,1536]{2,0,1:T(8,128)(2,1)S(1)} %get-tuple-element.11, bf16[256,1,1536]{2,0,1:T(8,128)(2,1)S(1)} %get-tuple-element.9), kind=kOutput, calls=%fused_computation.10 | convolution fusion | flops 1814298624 | bytes 10223616 | tf_op jit(solution)/shard_map/tkc,cko->to/dot_general | solution.py:51
  25.1 1.7 %convolution_convert_fusion = bf16[256,1536]{1,0:T(8,128)(2,1)} fusion(bf16[1536,768]{1,0:T(8,128)(2,1)S(1)} %copy-done, f32[256,768]{1,0:T(8,128)S(1)} %fusion.7), kind=kOutput, calls=%fused_computation.3 | convolution fusion | flops 606142464 | bytes 3932160 | tf_op jit(solution)/shard_map/tc,oc->to/dot_general | solution.py:56
  27.0 2.4 %all_gather.7 = bf16[256,1536]{1,0:T(8,128)(2,1)S(1)} all-gather(bf16[256,768]{1,0:T(8,128)(2,1)S(1)} %copy-done.3), channel_id=1, replica_groups=mesh['groups'=2,'seq'=8,'tensor'=2] {'tensor'}, dimensions={1}, use_global_device_ids=true | all-gather | bytes 1179648 | tf_op jit(solution)/shard_map/all_gather | solution.py:61
  29.3 2.2 %fusion.10 = bf16[256,768]{1,0:T(8,128)(2,1)S(1)} fusion(bf16[256,1536]{1,0:T(8,128)(2,1)S(1)} %all_gather.7, bf16[1536,768]{1,0:T(8,128)(2,1)S(1)} %copy-done, f32[256,768]{1,0:T(8,128)} %copy-done.1), kind=kOutput, calls=%fused_computation.12 | convolution fusion | flops 607715328 | bytes 4325376 | tf_op jit(solution)/shard_map/dot_general | solution.py:62
  31.5 1.3 collective-permute-start.2
  32.8 5.0 %collective-permute-start.3 = (bf16[32,768]{1,0:T(8,128)(2,1)S(1)}, bf16[32,768]{1,0:T(8,128)(2,1)S(1)}, u32[]{:S(2)}, u32[]{:S(2)}) collective-permute-start(bf16[32,768]{1,0:T(8,128)(2,1)S(1)} %get-tuple-element.15), channel_id=1, source_target_pairs={{0,2},{2,4},{4,6},{6,8},{8,10},{10,12},{12,14},{1,3},{3,5},{5,7},{... | collective-permute-start | bytes 147464 | tf_op jit(solution)/shard_map/ppermute | solution.py:20
  37.8 0.1 collective-permute-done.2
  37.9 1.6 collective-permute-done.3
  39.5 0.1 fusion.22
  39.6 5.9 %fusion = bf16[256,1536]{1,0:T(8,128)(2,1)} fusion(bf16[1536,3,768]{2,0,1:T(8,128)(2,1)} %param.5, bf16[256,1,768]{2,0,1:T(8,128)(2,1)S(1)} %get-tuple-element.13, bf16[256,1,768]{2,0,1:T(8,128)(2,1)S(1)} %bitcast.26, bf16[256,1,768]{2,0,1:T(8,128)(2,1)S(1)} %get-tuple-element.12), kind=kOutput, calls=%fused_computation.2 | convolution fusion | flops 1813512192 | bytes 9043968 | tf_op jit(solution)/shard_map/tko,cko->tc/dot_general | solution.py:75
  45.6 4.2 %convolution_bitcast_fusion = f32[1536,768]{0,1:T(8,128)} fusion(bf16[256,1536]{1,0:T(8,128)(2,1)S(1)} %all_gather.7, f32[256,768]{1,0:T(8,128)} %copy-done.1), kind=kOutput, calls=%fused_computation | convolution fusion | flops 605749248 | bytes 6291456 | tf_op jit(solution)/shard_map/to,tc->oc/dot_general | solution.py:81
  49.8 6.1 %copy.9 = f32[1536,768]{1,0:T(8,128)} copy(f32[1536,768]{0,1:T(8,128)} %convolution_bitcast_fusion) | data formatting | bytes 9437184
  55.9 1.0 copy-done.2
  56.8 1.8 %add_convert_fusion.1 = bf16[256,768]{1,0:T(8,128)(2,1)} fusion(bf16[256,768]{1,0:T(8,128)(2,1)} %reduce-scatter.6.cloned.1.call-done, bf16[256,768]{1,0:T(8,128)(2,1)S(1)} %copy-done.2), kind=kLoop, calls=%fused_computation.29 | loop fusion | flops 786432 | bytes 1179648 | tf_op jit(solution)/shard_map/convert_element_type | solution.py:60
  58.7 1.8 %add_convert_fusion = bf16[256,768]{1,0:T(8,128)(2,1)} fusion(bf16[256,768]{1,0:T(8,128)(2,1)} %reduce-scatter.8.cloned.1.call-done, bf16[256,768]{1,0:T(8,128)(2,1)S(1)} %copy-done.3), kind=kLoop, calls=%fused_computation.28 | loop fusion | flops 786432 | bytes 1179648 | tf_op jit(solution)/shard_map/convert_element_type | solution.py:79
  60.5 97.6 %reduce-scatter.10.cloned.1.call-done = f32[192,768]{1,0:T(8,128)} async-done(((f32[1536,768]{1,0:T(8,128)}), f32[192,768]{1,0:T(8,128)}) %reduce-scatter.10.cloned.1.call-update) | async-done | bytes 589840
  (18 shorter events, 0.2 us)
Async XLA Ops:
  7.2 17.9 %copy-start = (bf16[1536,768]{1,0:T(8,128)(2,1)S(1)}, bf16[1536,768]{1,0:T(8,128)(2,1)}, u32[]{:S(2)}) copy-start(bf16[1536,768]{1,0:T(8,128)(2,1)} %param.6) | copy-start | bytes 7077892
  7.2 48.7 %reduce-scatter.6.cloned.1.call-start = ((), (), s32[]{:S(2)}) async-start(), calls=%async_computation.3 | async-start | bytes 1179648 | tf_op jit(solution)/shard_map/reduce_scatter | solution.py:57
  8.2 6.6 %collective-permute-start = (bf16[32,768]{1,0:T(8,128)(2,1)S(1)}, bf16[32,768]{1,0:T(8,128)(2,1)S(1)}, u32[]{:S(2)}, u32[]{:S(2)}) collective-permute-start(bf16[32,768]{1,0:T(8,128)(2,1)S(1)} %get-tuple-element.16), channel_id=1, source_target_pairs={{0,2},{2,4},{4,6},{6,8},{8,10},{10,12},{12,14},{1,3},{3,5},{5,7},{... | collective-permute-start | bytes 147464 | tf_op jit(solution)/shard_map/ppermute | solution.py:20
  13.1 6.0 %collective-permute-start.1 = (bf16[32,768]{1,0:T(8,128)(2,1)S(1)}, bf16[32,768]{1,0:T(8,128)(2,1)S(1)}, u32[]{:S(2)}, u32[]{:S(2)}) collective-permute-start(bf16[32,768]{1,0:T(8,128)(2,1)S(1)} %get-tuple-element.17), channel_id=1, source_target_pairs={{2,0},{4,2},{6,4},{8,6},{10,8},{12,10},{14,12},{3,1},{5,3},{7,5},{... | collective-permute-start | bytes 147464 | tf_op jit(solution)/shard_map/ppermute | solution.py:23
  19.1 4.0 %copy-start.4 = (bf16[1536,3,768]{2,0,1:T(8,128)(2,1)S(1)}, bf16[1536,3,768]{2,0,1:T(8,128)(2,1)}, u32[]{:S(2)}) copy-start(bf16[1536,3,768]{2,0,1:T(8,128)(2,1)} %param.5) | copy-start | bytes 21233668
  25.1 1.8 %copy-start.1 = (f32[256,768]{1,0:T(8,128)}, f32[256,768]{1,0:T(8,128)S(1)}, u32[]{:S(2)}) copy-start(f32[256,768]{1,0:T(8,128)S(1)} %fusion.7) | copy-start | bytes 2359300
  25.1 1.8 %copy-start.3 = (bf16[256,768]{1,0:T(8,128)(2,1)S(1)}, bf16[256,768]{1,0:T(8,128)(2,1)}, u32[]{:S(2)}) copy-start(bf16[256,768]{1,0:T(8,128)(2,1)} %param.7) | copy-start | bytes 1179652
  26.9 31.8 %reduce-scatter.8.cloned.1.call-start = ((), (), s32[]{:S(2)}) async-start(), calls=%async_computation.4 | async-start | bytes 1179648 | tf_op jit(solution)/shard_map/reduce_scatter | solution.py:76
  31.5 6.4 %collective-permute-start.2 = (bf16[32,768]{1,0:T(8,128)(2,1)S(1)}, bf16[32,768]{1,0:T(8,128)(2,1)S(1)}, u32[]{:S(2)}, u32[]{:S(2)}) collective-permute-start(bf16[32,768]{1,0:T(8,128)(2,1)S(1)} %get-tuple-element.14), channel_id=1, source_target_pairs={{2,0},{4,2},{6,4},{8,6},{10,8},{12,10},{14,12},{3,1},{5,3},{7,5},{... | collective-permute-start | bytes 147464 | tf_op jit(solution)/shard_map/ppermute | solution.py:23
  32.8 6.7 %collective-permute-start.3 = (bf16[32,768]{1,0:T(8,128)(2,1)S(1)}, bf16[32,768]{1,0:T(8,128)(2,1)S(1)}, u32[]{:S(2)}, u32[]{:S(2)}) collective-permute-start(bf16[32,768]{1,0:T(8,128)(2,1)S(1)} %get-tuple-element.15), channel_id=1, source_target_pairs={{0,2},{2,4},{4,6},{6,8},{8,10},{10,12},{12,14},{1,3},{3,5},{5,7},{... | collective-permute-start | bytes 147464 | tf_op jit(solution)/shard_map/ppermute | solution.py:20
  45.5 112.6 %reduce-scatter.10.cloned.1.call-start = ((), (), s32[]{:S(2)}) async-start(), calls=%async_computation.5 | async-start | bytes 5308416
  55.8 1.0 copy-start.2
Sparse Core Ops, SparseCore 0:
  27.0 9.3 reduce-scatter.5
  45.6 11.6 reduce-scatter.7
  61.5 96.5 reduce-scatter.9
where the time goes:
time: 165 us
  waiting for transfers between devices  104 us (63%)
  matrix products  16 us (10%)
  between operations  13.9 us (8%)
  starting transfers between devices  12.5 us (8%)
  local copies, waits for them, and re-layouts  8.21 us (5%)
  blocking collectives  5.01 us (3%)
  other arithmetic  4.91 us (3%)
    unnamed x4, waiting for transfers between devices  97.7 us
    ppermute x2, starting transfers between devices, extended(): lax.ppermute(lax.slice_in_dim(block, block.shape[dim] - width, None, axis...  9.81 us
    unnamed x11, local copies, waits for them, and re-layouts  7.04 us
    dot_general x1, matrix products, local(): jnp.einsum('tko,cko->tc', back_taps, w_dilated, preferred_element_type=jn...  5.93 us
    ppermute x2, waiting for transfers between devices, extended(): lax.ppermute(lax.slice_in_dim(block, 0, width, axis=dim), axis, backward)  4.38 us
    dot_general x1, matrix products, local(): jnp.einsum('to,tc->oc', full_grad, activation, preferred_element_type=jnp...  4.22 us
  transfers between devices with their start and end apart: 7, of which 5 were waited for; matrix products, arithmetic and copies ran while one was open for 13% of the time, Pallas kernels for 0%

commit v1 on v0

v1 whole, which is shorter than its diff:
```python
import functools
import math

import jax
import jax.numpy as jnp
from jax import lax
from jax.experimental import pallas as pl
from jax.experimental.pallas import tpu as pltpu
from jax.sharding import PartitionSpec as P

DILATION_BINS = 32
MESH = pl.DeviceIdType.MESH

gelu_cubic = 0.044715
gelu_scale = math.sqrt(2.0 / math.pi)


def gelu_pair(values):
    square = values * values
    tangent = jnp.tanh(gelu_scale * (values + gelu_cubic * square * values))
    half = 0.5 * (1.0 + tangent)
    slope = half + 0.5 * values * (1.0 - tangent * tangent) * gelu_scale * (
        1.0 + 3.0 * gelu_cubic * square
    )
    return values * half, slope


def dot_nn(a, b):
    return jnp.dot(a, b, preferred_element_type=jnp.float32)


def dot_nt(a, b):
    return lax.dot_general(a, b, (((1,), (1,)), ((), ())), preferred_element_type=jnp.float32)


def kernel(n, tile, with_point, *refs):
    x_ref, w_hbm, p_hbm, d_ref = refs[:4]
    if with_point:
        out_ref, gi_ref, gp_ref = refs[4:7]
        act, dfull = refs[7:9]
        rest = refs[9:]
    else:
        out_ref, gi_ref, act, dfull = refs[4:8]
        rest = refs[8:]
    (w, p, xfull, slope, ghpad, msend, mrecv, bsend, brecv) = rest[:9]
    (lsem, ssem, rsem, xs_sem, xr_sem, gs_sem, gr_sem) = rest[9:16]
    if with_point:
        (actp, dp, dps, cot_t, gps, gpr, as_sem, ar_sem, ps_sem, pr_sem) = rest[16:]

    s = lax.axis_index("seq")
    t = lax.axis_index("tensor")
    o = 1 - t
    T, H = x_ref.shape
    C = 2 * H
    R = DILATION_BINS
    tiles = H // tile
    bf16 = jnp.bfloat16
    has_low = s > 0
    has_high = s < n - 1
    mine = pl.ds(pl.multiple_of(t * H, H), H)
    other = pl.ds(pl.multiple_of(o * H, H), H)
    nz = n // 2
    z = s // 2
    y = lax.rem(s, 2)
    pair = s + 1 - 2 * y

    def remote(src, dst, send, recv, seq, tensor):
        return pltpu.make_async_remote_copy(
            src_ref=src,
            dst_ref=dst,
            send_sem=send,
            recv_sem=recv,
            device_id={"seq": seq, "tensor": tensor},
            device_id_type=MESH,
        )

    def cols(j):
        return pl.ds(pl.multiple_of(j * tile, tile), tile)

    w_loads = [pltpu.make_async_copy(w_hbm.at[k], w.at[k], lsem.at[k]) for k in range(3)]
    p_load = pltpu.make_async_copy(p_hbm, p, lsem.at[3])
    for load in w_loads:
        load.start()
    p_load.start()

    barrier = pltpu.get_barrier_semaphore()

    def greet(seq, tensor):
        pl.semaphore_signal(
            barrier, inc=1, device_id={"seq": seq, "tensor": tensor}, device_id_type=MESH
        )

    greet(s, o)

    @pl.when(has_low)
    def _():
        greet(s - 1, t)
        greet(s - 1, o)

    @pl.when(has_high)
    def _():
        greet(s + 1, t)
        greet(s + 1, o)

    if with_point:
        for d in range(1, nz):
            greet(lax.rem(z + d, nz) * 2 + y, t)
    xfull[pl.ds(R, T), mine] = x_ref[...]
    dfull[:, mine] = d_ref[...]
    sides = lax.div(s + n - 1, n) + lax.div(2 * n - 2 - s, n)
    pl.semaphore_wait(barrier, 1 + (nz - 1 if with_point else 0) + 2 * sides)

    def to_low(slot, tensor):
        return remote(
            x_ref.at[pl.ds(0, R), :], xfull.at[pl.ds(R + T, R), mine],
            xs_sem.at[slot], xr_sem.at[2 + t], s - 1, tensor,
        )

    def to_high(slot, tensor):
        return remote(
            x_ref.at[pl.ds(T - R, R), :], xfull.at[pl.ds(0, R), mine],
            xs_sem.at[2 + slot], xr_sem.at[t], s + 1, tensor,
        )

    @pl.when(has_low)
    def _():
        to_low(0, t).start()
        to_low(1, o).start()

    @pl.when(has_high)
    def _():
        to_high(0, t).start()
        to_high(1, o).start()

    x_side = remote(x_ref, xfull.at[pl.ds(R, T), mine], ssem.at[0], rsem.at[0], s, o)
    x_side.start()
    d_side = remote(d_ref, dfull.at[:, mine], ssem.at[1], rsem.at[1], s, o)
    d_side.start()
    if with_point:
        d_pair = remote(d_ref, dp, ssem.at[2], rsem.at[2], pair, t)
        d_pair.start()
        d_next = remote(dp, dps, ssem.at[3], rsem.at[3], s, o)
        cot_t[mine, pl.ds(0, T)] = d_ref[...].T

    @pl.when(s == 0)
    def _():
        xfull[pl.ds(0, R), :] = jnp.zeros((R, C), bf16)
        ghpad[pl.ds(0, R), :] = jnp.zeros((R, H), bf16)

    @pl.when(s == n - 1)
    def _():
        xfull[pl.ds(R + T, R), :] = jnp.zeros((R, C), bf16)
        ghpad[pl.ds(R + T, R), :] = jnp.zeros((R, H), bf16)

    remote(x_ref, xfull.at[pl.ds(R, T), other], ssem.at[0], rsem.at[0], s, o).wait_recv()

    @pl.when(has_low)
    def _():
        for half in range(2):
            remote(
                x_ref.at[pl.ds(0, R), :], xfull.at[pl.ds(0, R), pl.ds(half * H, H)],
                xs_sem.at[0], xr_sem.at[half], s - 1, t,
            ).wait_recv()

    @pl.when(has_high)
    def _():
        for half in range(2):
            remote(
                x_ref.at[pl.ds(0, R), :], xfull.at[pl.ds(R + T, R), pl.ds(half * H, H)],
                xs_sem.at[0], xr_sem.at[2 + half], s + 1, t,
            ).wait_recv()

    for load in w_loads:
        load.wait()

    def act_copy(j):
        return remote(
            act.at[j], actp.at[j], as_sem.at[j], ar_sem.at[j], pair, t
        )

    @pl.loop(0, tiles)
    def _(j):
        hidden = dot_nn(xfull[pl.ds(0, T), :], w[0, :, cols(j)])
        hidden += dot_nn(xfull[pl.ds(R, T), :], w[1, :, cols(j)])
        hidden += dot_nn(xfull[pl.ds(2 * R, T), :], w[2, :, cols(j)])
        value, derivative = gelu_pair(hidden)
        act[j] = value.astype(bf16)
        slope[:, cols(j)] = derivative
        if with_point:
            act_copy(j).start()

    if with_point:
        remote(d_ref, dp, ssem.at[2], rsem.at[2], pair, t).wait_recv()
        d_next.start()
        cot_t[mine, pl.ds(T, T)] = dp[...].T
    remote(d_ref, dfull.at[:, other], ssem.at[1], rsem.at[1], s, o).wait_recv()
    p_load.wait()
    if with_point:
        cot_t[other, pl.ds(0, T)] = dfull[:, other].T

    @pl.loop(0, tiles)
    def _(j):
        grad = dot_nn(dfull[...], p[:, cols(j)]) * slope[:, cols(j)]
        ghpad[pl.ds(R, T), cols(j)] = grad.astype(bf16)

    gh_low = remote(
        ghpad.at[pl.ds(R, R), :], ghpad.at[pl.ds(R + T, R), :],
        gs_sem.at[0], gr_sem.at[1], s - 1, t,
    )
    gh_high = remote(
        ghpad.at[pl.ds(T, R), :], ghpad.at[pl.ds(0, R), :],
        gs_sem.at[1], gr_sem.at[0], s + 1, t,
    )

    @pl.when(has_low)
    def _():
        gh_low.start()

    @pl.when(has_high)
    def _():
        gh_high.start()

    def point_copy(d, j):
        return remote(
            gps.at[d - 1, j], gpr.at[d - 1, j], ps_sem.at[d - 1, j], pr_sem.at[d - 1, j],
            lax.rem(z + d, nz) * 2 + y, t,
        )

    if with_point:
        rows = gp_ref.shape[0]
        remote(dp, dps, ssem.at[3], rsem.at[3], s, o).wait_recv()
        cot_t[other, pl.ds(T, T)] = dps[...].T

        @pl.loop(0, tiles)
        def _(j):
            act_copy(j).wait_recv()

            def block(d):
                owner = lax.rem(z + d, nz) * 2 + y
                at = pl.ds(pl.multiple_of(owner * rows, rows), rows)
                return dot_nn(cot_t[at, pl.ds(0, T)], act[j]) + dot_nn(
                    cot_t[at, pl.ds(T, T)], actp[j]
                )

            for d in range(1, nz):
                gps[d - 1, j] = block(d).astype(bf16)
                point_copy(d, j).start()
            gp_ref[:, cols(j)] = block(0)

    def mixed(at):
        total = dot_nt(act[0], p[at, pl.ds(0, tile)])
        for i in range(1, tiles):
            total += dot_nt(act[i], p[at, pl.ds(i * tile, tile)])
        return total.astype(bf16)

    @pl.loop(0, tiles)
    def _(j):
        msend[:, cols(j)] = mixed(pl.ds(pl.multiple_of(o * H + j * tile, tile), tile))

    m_side = remote(msend, mrecv, ssem.at[4], rsem.at[4], s, o)
    m_side.start()

    @pl.when(has_low)
    def _():
        remote(
            ghpad.at[pl.ds(R, R), :], ghpad.at[pl.ds(0, R), :],
            gs_sem.at[0], gr_sem.at[0], s - 1, t,
        ).wait_recv()

    @pl.when(has_high)
    def _():
        remote(
            ghpad.at[pl.ds(R, R), :], ghpad.at[pl.ds(R + T, R), :],
            gs_sem.at[0], gr_sem.at[1], s + 1, t,
        ).wait_recv()

    def back(at):
        total = dot_nt(ghpad[pl.ds(2 * R, T), :], w[0, at, :])
        total += dot_nt(ghpad[pl.ds(R, T), :], w[1, at, :])
        total += dot_nt(ghpad[pl.ds(0, T), :], w[2, at, :])
        return total.astype(bf16)

    @pl.loop(0, tiles)
    def _(j):
        bsend[:, cols(j)] = back(pl.ds(pl.multiple_of(o * H + j * tile, tile), tile))

    b_side = remote(bsend, brecv, ssem.at[5], rsem.at[5], s, o)
    b_side.start()
    m_side.wait_recv()

    @pl.loop(0, tiles)
    def _(j):
        own = mixed(pl.ds(pl.multiple_of(t * H + j * tile, tile), tile))
        total = x_ref[:, cols(j)].astype(jnp.float32) + own.astype(jnp.float32)
        out_ref[:, cols(j)] = (total + mrecv[:, cols(j)].astype(jnp.float32)).astype(bf16)

    b_side.wait_recv()

    @pl.loop(0, tiles)
    def _(j):
        own = back(pl.ds(pl.multiple_of(t * H + j * tile, tile), tile))
        total = d_ref[:, cols(j)].astype(jnp.float32) + own.astype(jnp.float32)
        gi_ref[:, cols(j)] = (total + brecv[:, cols(j)].astype(jnp.float32)).astype(bf16)

    if with_point:

        @pl.loop(0, tiles)
        def _(j):
            total = gp_ref[:, cols(j)]
            for d in range(1, nz):
                point_copy(d, j).wait_recv()
                total += gpr[d - 1, j].astype(jnp.float32)
            gp_ref[:, cols(j)] = total

    @pl.when(has_low)
    def _():
        to_low(0, t).wait_send()
        to_low(1, o).wait_send()
        gh_low.wait_send()

    @pl.when(has_high)
    def _():
        to_high(0, t).wait_send()
        to_high(1, o).wait_send()
        gh_high.wait_send()

    x_side.wait_send()
    d_side.wait_send()
    m_side.wait_send()
    b_side.wait_send()
    if with_point:
        d_pair.wait_send()
        d_next.wait_send()

        @pl.loop(0, tiles)
        def _(j):
            act_copy(j).wait_send()
            for d in range(1, nz):
                point_copy(d, j).wait_send()


def local(n, inputs, w_dilated, w_point, cotangent):
    T, H = inputs.shape
    C = w_point.shape[0]
    R = DILATION_BINS
    tile = 256
    tiles = H // tile
    rows = C // n
    bf16, f32 = jnp.bfloat16, jnp.float32
    with_point = rows % 16 == 0 and n % 2 == 0
    nz = n // 2
    vmem = pl.BlockSpec(memory_space=pltpu.VMEM)
    hbm = pl.BlockSpec(memory_space=pl.ANY)
    plane = jax.ShapeDtypeStruct((T, H), bf16)
    act_shape = (tiles, T, tile)
    outs = [plane, plane]
    scratch = []
    if with_point:
        outs += [jax.ShapeDtypeStruct((rows, H), f32)]
        scratch += [pltpu.VMEM(act_shape, bf16), pltpu.VMEM((T, C), bf16)]
    else:
        outs += [jax.ShapeDtypeStruct(act_shape, bf16), jax.ShapeDtypeStruct((T, C), bf16)]
    dma = pltpu.SemaphoreType.DMA
    scratch += [
        pltpu.VMEM((3, C, H), bf16),
        pltpu.VMEM((C, H), bf16),
        pltpu.VMEM((T + 2 * R, C), bf16),
        pltpu.VMEM((T, H), f32),
        pltpu.VMEM((T + 2 * R, H), bf16),
        pltpu.VMEM((T, H), bf16),
        pltpu.VMEM((T, H), bf16),
        pltpu.VMEM((T, H), bf16),
        pltpu.VMEM((T, H), bf16),
        dma((4,)), dma((6,)), dma((6,)), dma((4,)), dma((4,)), dma((2,)), dma((2,)),
    ]
    if with_point:
        scratch += [
            pltpu.VMEM(act_shape, bf16),
            pltpu.VMEM((T, H), bf16),
            pltpu.VMEM((T, H), bf16),
            pltpu.VMEM((C, 2 * T), bf16),
            pltpu.VMEM((nz - 1, tiles, rows, tile), bf16),
            pltpu.VMEM((nz - 1, tiles, rows, tile), bf16),
            dma((tiles,)), dma((tiles,)), dma((nz - 1, tiles)), dma((nz - 1, tiles)),
        ]
    results = pl.pallas_call(
        functools.partial(kernel, n, tile, with_point),
        out_shape=outs,
        in_specs=[vmem, hbm, hbm, vmem],
        out_specs=[vmem] * len(outs),
        scratch_shapes=scratch,
        compiler_params=pltpu.CompilerParams(
            collective_id=0, has_side_effects=True, vmem_limit_bytes=48 * 1024 * 1024
        ),
    )(inputs, jnp.transpose(w_dilated, (1, 0, 2)), w_point, cotangent)
    if with_point:
        return tuple(results)
    output, grad_inputs, act, full_grad = results
    activation = jnp.transpose(act, (1, 0, 2)).reshape(T, H)
    grad_point = lax.psum_scatter(
        jnp.einsum("to,tc->oc", full_grad, activation, preferred_element_type=f32),
        "seq",
        scatter_dimension=0,
        tiled=True,
    )
    return (output, grad_inputs, grad_point)


def solution(mesh):
    placed = (
        P(("groups", "seq"), "tensor"),
        P(None, None, "tensor"),
        P(None, "tensor"),
        P(("groups", "seq"), "tensor"),
    )
    return jax.shard_map(
        functools.partial(local, mesh.shape["seq"]),
        mesh=mesh,
        in_specs=placed,
        out_specs=(
            P(("groups", "seq"), "tensor"),
            P(("groups", "seq"), "tensor"),
            P(("groups", "seq"), "tensor"),
        ),
        check_vma=False,
    )
```

time: 165 us -> 55.6 us (0.34)
  waiting for transfers between devices: 104 us -> 0 us
  Pallas kernels: 0 us -> 48.8 us
  matrix products: 16 us -> 0 us
  between operations: 13.9 us -> 0.65 us
  starting transfers between devices: 12.5 us -> 0 us
  blocking collectives: 5.01 us -> 0 us
  other arithmetic: 4.91 us -> 0 us
  local copies, waits for them, and re-layouts: 8.21 us -> 5.96 us
    unnamed x4 -> x0, waiting for transfers between devices: 97.7 us -> none
    pallas_call x0 -> x1, Pallas kernels: none -> 48.8 us  [local(): pl.pallas_call(functools.partial(kernel, n, tile, with_point), out_shape=...]
    dot_general x5 -> x0, matrix products: 16 us -> none  [the longest x1 5.93 us: local(): jnp.einsum('tko,cko->tc', back_taps, w_dilated, preferred_element_type=jn...]
    ppermute x4 -> x0, starting transfers between devices: 12.4 us -> none  [the longest x2 9.81 us: extended(): lax.ppermute(lax.slice_in_dim(block, block.shape[dim] - width, None, axis...]
    ppermute x4 -> x0, waiting for transfers between devices: 6.41 us -> none  [the longest x2 4.38 us: extended(): lax.ppermute(lax.slice_in_dim(block, 0, width, axis=dim), axis, backward)]
    all_gather x2 -> x0, blocking collectives: 5.01 us -> none  [the longest x1 2.64 us: local(): padded_input = lax.all_gather(rimmed, 'tensor', axis=1, tiled=True)]
    convert_element_type x2 -> x0, other arithmetic: 3.67 us -> none  [the longest x1 1.84 us: local(): output = (inputs.astype(jnp.float32) + mixed_sum).astype(jnp.bfloat16)]
    unnamed x11 -> x9, local copies, waits for them, and re-layouts: 7.04 us -> 5.96 us
  transfers between devices with their start and end apart: 7 -> 0, of which waited for: 5 -> 0; matrix products, arithmetic and copies ran while one was open for 13% -> 0% of each run, Pallas kernels for 0% -> 0%
where the time goes in v1:
time: 55.6 us; the launch traced here: 55.4 us
  Pallas kernels  48.8 us (88%)
  local copies, waits for them, and re-layouts  5.96 us (11%)
  between operations  0.65 us (1%)
    pallas_call x1, Pallas kernels, local(): pl.pallas_call(functools.partial(kernel, n, tile, with_point), out_shape=...  48.8 us
    unnamed x9, local copies, waits for them, and re-layouts  5.96 us

profile of v1, /device:TPU:0, one launch (start us, length us, event | category | flops | bytes accessed | tf_op | source)
XLA Modules:
  0.0 55.4 jit_solution(3043269904716571669)
XLA Ops:
  0.6 0.0 copy-start
  0.6 1.7 %copy-done = bf16[1536,768]{1,0:T(8,128)(2,1)S(1)} copy-done((bf16[1536,768]{1,0:T(8,128)(2,1)S(1)}, bf16[1536,768]{1,0:T(8,128)(2,1)}, u32[]{:S(2)}) %copy-start) | copy-done | bytes 2359320
  2.3 0.0 copy-start.1
  2.3 1.0 %copy-done.1 = bf16[256,768]{1,0:T(8,128)(2,1)S(1)} copy-done((bf16[256,768]{1,0:T(8,128)(2,1)S(1)}, bf16[256,768]{1,0:T(8,128)(2,1)}, u32[]{:S(2)}) %copy-start.1) | copy-done | bytes 393240
  3.3 0.0 copy-start.2
  3.3 1.0 %copy-done.2 = bf16[256,768]{1,0:T(8,128)(2,1)S(1)} copy-done((bf16[256,768]{1,0:T(8,128)(2,1)S(1)}, bf16[256,768]{1,0:T(8,128)(2,1)}, u32[]{:S(2)}) %copy-start.2) | copy-done | bytes 393240
  4.3 48.8 %shard_map.67 = (bf16[256,768]{1,0:T(8,128)(2,1)S(1)}, bf16[256,768]{1,0:T(8,128)(2,1)S(1)}, f32[192,768]{1,0:T(8,128)S(1)}) custom-call(bf16[256,768]{1,0:T(8,128)(2,1)S(1)} %copy-done.1, bf16[3,1536,768]{2,1,0:T(8,128)(2,1)} %bitcast.1, bf16[1536,768]{1,0:T(8,128)(2,1)S(1)} %copy-done, bf16[256,768]{1,0:T(8,128)(2,1)S(1)} %copy-done.2), custom_call_target="tpu_custom_call" | custom-call | tf_op jit(solution)/shard_map/pallas_call | solution.py:386
  53.1 0.7 %copy.10 = bf16[256,768]{1,0:T(8,128)(2,1)} copy(bf16[256,768]{1,0:T(8,128)(2,1)S(1)} %get-tuple-element.6) | data formatting | bytes 786432
  53.9 0.7 %copy.11 = bf16[256,768]{1,0:T(8,128)(2,1)} copy(bf16[256,768]{1,0:T(8,128)(2,1)S(1)} %get-tuple-element.7) | data formatting | bytes 786432
  54.6 0.8 %copy.12 = f32[192,768]{1,0:T(8,128)} copy(f32[192,768]{1,0:T(8,128)S(1)} %get-tuple-element.8) | data formatting | bytes 1179648
Async XLA Ops:
  0.6 1.7 %copy-start = (bf16[1536,768]{1,0:T(8,128)(2,1)S(1)}, bf16[1536,768]{1,0:T(8,128)(2,1)}, u32[]{:S(2)}) copy-start(bf16[1536,768]{1,0:T(8,128)(2,1)} %refs_2_.1) | copy-start | bytes 7077892
  2.3 1.0 %copy-start.1 = (bf16[256,768]{1,0:T(8,128)(2,1)S(1)}, bf16[256,768]{1,0:T(8,128)(2,1)}, u32[]{:S(2)}) copy-start(bf16[256,768]{1,0:T(8,128)(2,1)} %refs_0_.1) | copy-start | bytes 1179652
  3.3 1.0 %copy-start.2 = (bf16[256,768]{1,0:T(8,128)(2,1)S(1)}, bf16[256,768]{1,0:T(8,128)(2,1)}, u32[]{:S(2)}) copy-start(bf16[256,768]{1,0:T(8,128)(2,1)} %refs_3_.1) | copy-start | bytes 1179652

commit v2 on v1

--- a/solution.py
+++ b/solution.py
@@ -34,7 +34,7 @@
 
 
 def kernel(n, tile, with_point, *refs):
-    x_ref, w_hbm, p_hbm, d_ref = refs[:4]
+    x_hbm, w_hbm, p_hbm, d_hbm = refs[:4]
     if with_point:
         out_ref, gi_ref, gp_ref = refs[4:7]
         act, dfull = refs[7:9]
@@ -50,7 +50,7 @@
     s = lax.axis_index("seq")
     t = lax.axis_index("tensor")
     o = 1 - t
-    T, H = x_ref.shape
+    T, H = x_hbm.shape
     C = 2 * H
     R = DILATION_BINS
     tiles = H // tile
@@ -77,10 +77,21 @@
     def cols(j):
         return pl.ds(pl.multiple_of(j * tile, tile), tile)
 
-    w_loads = [pltpu.make_async_copy(w_hbm.at[k], w.at[k], lsem.at[k]) for k in range(3)]
-    p_load = pltpu.make_async_copy(p_hbm, p, lsem.at[3])
-    for load in w_loads:
-        load.start()
+    x_ref = xfull.at[pl.ds(R, T), mine]
+    d_ref = dfull.at[:, mine]
+    x_load = pltpu.make_async_copy(x_hbm, x_ref, lsem.at[0])
+    d_load = pltpu.make_async_copy(d_hbm, d_ref, lsem.at[1])
+    p_load = pltpu.make_async_copy(p_hbm, p, lsem.at[2])
+    x_load.start()
+    d_load.start()
+
+    def w_load(j):
+        return pltpu.make_async_copy(
+            w_hbm.at[:, :, cols(j)], w.at[:, :, cols(j)], lsem.at[3 + j]
+        )
+
+    for j in range(tiles):
+        w_load(j).start()
     p_load.start()
 
     barrier = pltpu.get_barrier_semaphore()
@@ -105,20 +116,18 @@
     if with_point:
         for d in range(1, nz):
             greet(lax.rem(z + d, nz) * 2 + y, t)
-    xfull[pl.ds(R, T), mine] = x_ref[...]
-    dfull[:, mine] = d_ref[...]
     sides = lax.div(s + n - 1, n) + lax.div(2 * n - 2 - s, n)
     pl.semaphore_wait(barrier, 1 + (nz - 1 if with_point else 0) + 2 * sides)
 
     def to_low(slot, tensor):
         return remote(
-            x_ref.at[pl.ds(0, R), :], xfull.at[pl.ds(R + T, R), mine],
+            x_hbm.at[pl.ds(0, R), :], xfull.at[pl.ds(R + T, R), mine],
             xs_sem.at[slot], xr_sem.at[2 + t], s - 1, tensor,
         )
 
     def to_high(slot, tensor):
         return remote(
-            x_ref.at[pl.ds(T - R, R), :], xfull.at[pl.ds(0, R), mine],
+            x_hbm.at[pl.ds(T - R, R), :], xfull.at[pl.ds(0, R), mine],
             xs_sem.at[2 + slot], xr_sem.at[t], s + 1, tensor,
         )
 
@@ -132,15 +141,18 @@
         to_high(0, t).start()
         to_high(1, o).start()
 
-    x_side = remote(x_ref, xfull.at[pl.ds(R, T), mine], ssem.at[0], rsem.at[0], s, o)
+    x_side = remote(x_hbm, xfull.at[pl.ds(R, T), mine], ssem.at[0], rsem.at[0], s, o)
     x_side.start()
-    d_side = remote(d_ref, dfull.at[:, mine], ssem.at[1], rsem.at[1], s, o)
+    d_side = remote(d_hbm, dfull.at[:, mine], ssem.at[1], rsem.at[1], s, o)
     d_side.start()
     if with_point:
-        d_pair = remote(d_ref, dp, ssem.at[2], rsem.at[2], pair, t)
+        d_pair = remote(d_hbm, dp, ssem.at[2], rsem.at[2], pair, t)
         d_pair.start()
         d_next = remote(dp, dps, ssem.at[3], rsem.at[3], s, o)
+        d_load.wait()
         cot_t[mine, pl.ds(0, T)] = d_ref[...].T
+    else:
+        d_load.wait()
 
     @pl.when(s == 0)
     def _():
@@ -152,13 +164,13 @@
         xfull[pl.ds(R + T, R), :] = jnp.zeros((R, C), bf16)
         ghpad[pl.ds(R + T, R), :] = jnp.zeros((R, H), bf16)
 
-    remote(x_ref, xfull.at[pl.ds(R, T), other], ssem.at[0], rsem.at[0], s, o).wait_recv()
+    remote(x_hbm, xfull.at[pl.ds(R, T), other], ssem.at[0], rsem.at[0], s, o).wait_recv()
 
     @pl.when(has_low)
     def _():
         for half in range(2):
             remote(
-                x_ref.at[pl.ds(0, R), :], xfull.at[pl.ds(0, R), pl.ds(half * H, H)],
+                x_hbm.at[pl.ds(0, R), :], xfull.at[pl.ds(0, R), pl.ds(half * H, H)],
                 xs_sem.at[0], xr_sem.at[half], s - 1, t,
             ).wait_recv()
 
@@ -166,12 +178,11 @@
     def _():
         for half in range(2):
             remote(
-                x_ref.at[pl.ds(0, R), :], xfull.at[pl.ds(R + T, R), pl.ds(half * H, H)],
+                x_hbm.at[pl.ds(0, R), :], xfull.at[pl.ds(R + T, R), pl.ds(half * H, H)],
                 xs_sem.at[0], xr_sem.at[2 + half], s + 1, t,
             ).wait_recv()
 
-    for load in w_loads:
-        load.wait()
+    x_load.wait()
 
     def act_copy(j):
         return remote(
@@ -180,6 +191,7 @@
 
     @pl.loop(0, tiles)
     def _(j):
+        w_load(j).wait()
         hidden = dot_nn(xfull[pl.ds(0, T), :], w[0, :, cols(j)])
         hidden += dot_nn(xfull[pl.ds(R, T), :], w[1, :, cols(j)])
         hidden += dot_nn(xfull[pl.ds(2 * R, T), :], w[2, :, cols(j)])
@@ -190,10 +202,10 @@
             act_copy(j).start()
 
     if with_point:
-        remote(d_ref, dp, ssem.at[2], rsem.at[2], pair, t).wait_recv()
+        remote(d_hbm, dp, ssem.at[2], rsem.at[2], pair, t).wait_recv()
         d_next.start()
         cot_t[mine, pl.ds(T, T)] = dp[...].T
-    remote(d_ref, dfull.at[:, other], ssem.at[1], rsem.at[1], s, o).wait_recv()
+    remote(d_hbm, dfull.at[:, other], ssem.at[1], rsem.at[1], s, o).wait_recv()
     p_load.wait()
     if with_point:
         cot_t[other, pl.ds(0, T)] = dfull[:, other].T
@@ -350,7 +362,7 @@
     with_point = rows % 16 == 0 and n % 2 == 0
     nz = n // 2
     vmem = pl.BlockSpec(memory_space=pltpu.VMEM)
-    hbm = pl.BlockSpec(memory_space=pl.ANY)
+    hbm = pl.BlockSpec(memory_space=pltpu.HBM)
     plane = jax.ShapeDtypeStruct((T, H), bf16)
     act_shape = (tiles, T, tile)
     outs = [plane, plane]
@@ -371,7 +383,7 @@
         pltpu.VMEM((T, H), bf16),
         pltpu.VMEM((T, H), bf16),
         pltpu.VMEM((T, H), bf16),
-        dma((4,)), dma((6,)), dma((6,)), dma((4,)), dma((4,)), dma((2,)), dma((2,)),
+        dma((3 + tiles,)), dma((6,)), dma((6,)), dma((4,)), dma((4,)), dma((2,)), dma((2,)),
     ]
     if with_point:
         scratch += [
@@ -386,11 +398,11 @@
     results = pl.pallas_call(
         functools.partial(kernel, n, tile, with_point),
         out_shape=outs,
-        in_specs=[vmem, hbm, hbm, vmem],
+        in_specs=[hbm] * 4,
         out_specs=[vmem] * len(outs),
         scratch_shapes=scratch,
         compiler_params=pltpu.CompilerParams(
-            collective_id=0, has_side_effects=True, vmem_limit_bytes=48 * 1024 * 1024
+            collective_id=0, has_side_effects=True, vmem_limit_bytes=60 * 1024 * 1024
         ),
     )(inputs, jnp.transpose(w_dilated, (1, 0, 2)), w_point, cotangent)
     if with_point:

time: 55.6 us -> 56.4 us (1.014)
  Pallas kernels: 48.8 us -> 50 us
    pallas_call x1, Pallas kernels: 48.8 us -> 50 us  [local(): pl.pallas_call(functools.partial(kernel, n, tile, with_point), out_shape=...]
    unnamed x9 -> x3, local copies, waits for them, and re-layouts: 5.96 us -> 5.45 us
where the time goes in v2:
time: 56.4 us; the launch traced here: 56.1 us
  Pallas kernels  50 us (89%)
  local copies, waits for them, and re-layouts  5.45 us (10%)
  between operations  0.64 us (1%)
    pallas_call x1, Pallas kernels, local(): pl.pallas_call(functools.partial(kernel, n, tile, with_point), out_shape=...  50 us
    unnamed x3, local copies, waits for them, and re-layouts  5.45 us

profile of v2, /device:TPU:0, one launch (start us, length us, event | category | flops | bytes accessed | tf_op | source)
XLA Modules:
  0.0 56.1 jit_solution(39387993494266984)
XLA Ops:
  0.6 50.0 %shard_map.67 = (bf16[256,768]{1,0:T(8,128)(2,1)}, bf16[256,768]{1,0:T(8,128)(2,1)}, f32[192,768]{1,0:T(8,128)}) custom-call(bf16[256,768]{1,0:T(8,128)(2,1)} %refs_0_.1, bf16[3,1536,768]{2,1,0:T(8,128)(2,1)} %bitcast.1, bf16[1536,768]{1,0:T(8,128)(2,1)} %refs_2_.1, bf16[256,768]{1,0:T(8,128)(2,1)} %refs_3_.1), custom_call_target="tpu_custom_call" | custom-call | tf_op jit(solution)/shard_map/pallas_call | solution.py:398
  50.7 1.8 %copy.10 = bf16[256,768]{1,0:T(8,128)(2,1)} copy(bf16[256,768]{1,0:T(8,128)(2,1)} %get-tuple-element.6) | data formatting | bytes 786432
  52.4 1.8 %copy.11 = bf16[256,768]{1,0:T(8,128)(2,1)} copy(bf16[256,768]{1,0:T(8,128)(2,1)} %get-tuple-element.7) | data formatting | bytes 786432
  54.2 1.9 %copy.12 = f32[192,768]{1,0:T(8,128)} copy(f32[192,768]{1,0:T(8,128)} %get-tuple-element.8) | data formatting | bytes 1179648

commit v3 on v2

--- a/solution.py
+++ b/solution.py
@@ -210,28 +210,6 @@
     if with_point:
         cot_t[other, pl.ds(0, T)] = dfull[:, other].T
 
-    @pl.loop(0, tiles)
-    def _(j):
-        grad = dot_nn(dfull[...], p[:, cols(j)]) * slope[:, cols(j)]
-        ghpad[pl.ds(R, T), cols(j)] = grad.astype(bf16)
-
-    gh_low = remote(
-        ghpad.at[pl.ds(R, R), :], ghpad.at[pl.ds(R + T, R), :],
-        gs_sem.at[0], gr_sem.at[1], s - 1, t,
-    )
-    gh_high = remote(
-        ghpad.at[pl.ds(T, R), :], ghpad.at[pl.ds(0, R), :],
-        gs_sem.at[1], gr_sem.at[0], s + 1, t,
-    )
-
-    @pl.when(has_low)
-    def _():
-        gh_low.start()
-
-    @pl.when(has_high)
-    def _():
-        gh_high.start()
-
     def point_copy(d, j):
         return remote(
             gps.at[d - 1, j], gpr.at[d - 1, j], ps_sem.at[d - 1, j], pr_sem.at[d - 1, j],
@@ -243,21 +221,42 @@
         remote(dp, dps, ssem.at[3], rsem.at[3], s, o).wait_recv()
         cot_t[other, pl.ds(T, T)] = dps[...].T
 
+        def block(d, j):
+            owner = lax.rem(z + d, nz) * 2 + y
+            at = pl.ds(pl.multiple_of(owner * rows, rows), rows)
+            return dot_nn(cot_t[at, pl.ds(0, T)], act[j]) + dot_nn(
+                cot_t[at, pl.ds(T, T)], actp[j]
+            )
+
         @pl.loop(0, tiles)
         def _(j):
             act_copy(j).wait_recv()
 
-            def block(d):
-                owner = lax.rem(z + d, nz) * 2 + y
-                at = pl.ds(pl.multiple_of(owner * rows, rows), rows)
-                return dot_nn(cot_t[at, pl.ds(0, T)], act[j]) + dot_nn(
-                    cot_t[at, pl.ds(T, T)], actp[j]
-                )
-
             for d in range(1, nz):
-                gps[d - 1, j] = block(d).astype(bf16)
+                gps[d - 1, j] = block(d, j).astype(bf16)
                 point_copy(d, j).start()
-            gp_ref[:, cols(j)] = block(0)
+
+    @pl.loop(0, tiles)
+    def _(j):
+        grad = dot_nn(dfull[...], p[:, cols(j)]) * slope[:, cols(j)]
+        ghpad[pl.ds(R, T), cols(j)] = grad.astype(bf16)
+
+    gh_low = remote(
+        ghpad.at[pl.ds(R, R), :], ghpad.at[pl.ds(R + T, R), :],
+        gs_sem.at[0], gr_sem.at[1], s - 1, t,
+    )
+    gh_high = remote(
+        ghpad.at[pl.ds(T, R), :], ghpad.at[pl.ds(0, R), :],
+        gs_sem.at[1], gr_sem.at[0], s + 1, t,
+    )
+
+    @pl.when(has_low)
+    def _():
+        gh_low.start()
+
+    @pl.when(has_high)
+    def _():
+        gh_high.start()
 
     def mixed(at):
         total = dot_nt(act[0], p[at, pl.ds(0, tile)])
@@ -318,7 +317,7 @@
 
         @pl.loop(0, tiles)
         def _(j):
-            total = gp_ref[:, cols(j)]
+            total = block(0, j)
             for d in range(1, nz):
                 point_copy(d, j).wait_recv()
                 total += gpr[d - 1, j].astype(jnp.float32)
@@ -402,7 +401,7 @@
         out_specs=[vmem] * len(outs),
         scratch_shapes=scratch,
         compiler_params=pltpu.CompilerParams(
-            collective_id=0, has_side_effects=True, vmem_limit_bytes=60 * 1024 * 1024
+            collective_id=0, has_side_effects=True, vmem_limit_bytes=58 * 1024 * 1024
         ),
     )(inputs, jnp.transpose(w_dilated, (1, 0, 2)), w_point, cotangent)
     if with_point:

time: 56.4 us -> 62.1 us (1.10)
  the two profiles are of different devices: /device:TPU:0 before, /device:TPU:13 now
where the time goes in v3:
time: 62.1 us; the launch traced here: 61.8 us
  Pallas kernels  55.8 us (90%)
  local copies, waits for them, and re-layouts  5.45 us (9%)
  between operations  0.64 us (1%)
    pallas_call x1, Pallas kernels, local(): pl.pallas_call(functools.partial(kernel, n, tile, with_point), out_shape=...  55.8 us
    unnamed x3, local copies, waits for them, and re-layouts  5.45 us

profile of v3, /device:TPU:13, one launch (start us, length us, event | category | flops | bytes accessed | tf_op | source)
XLA Modules:
  0.0 61.8 jit_solution(14996160178998045508)
XLA Ops:
  0.6 55.8 %shard_map.67 = (bf16[256,768]{1,0:T(8,128)(2,1)}, bf16[256,768]{1,0:T(8,128)(2,1)}, f32[192,768]{1,0:T(8,128)}) custom-call(bf16[256,768]{1,0:T(8,128)(2,1)} %refs_0_.1, bf16[3,1536,768]{2,1,0:T(8,128)(2,1)} %bitcast.1, bf16[1536,768]{1,0:T(8,128)(2,1)} %refs_2_.1, bf16[256,768]{1,0:T(8,128)(2,1)} %refs_3_.1), custom_call_target="tpu_custom_call" | custom-call | tf_op jit(solution)/shard_map/pallas_call | solution.py:397
  56.4 1.8 %copy.10 = bf16[256,768]{1,0:T(8,128)(2,1)} copy(bf16[256,768]{1,0:T(8,128)(2,1)} %get-tuple-element.6) | data formatting | bytes 786432
  58.2 1.8 %copy.11 = bf16[256,768]{1,0:T(8,128)(2,1)} copy(bf16[256,768]{1,0:T(8,128)(2,1)} %get-tuple-element.7) | data formatting | bytes 786432
  59.9 1.9 %copy.12 = f32[192,768]{1,0:T(8,128)} copy(f32[192,768]{1,0:T(8,128)} %get-tuple-element.8) | data formatting | bytes 1179648
